TPU v7x, 256 devices: a whole 4x4x8 slice. The times are simulated.
256 devices in a mesh: grp: 8 (over z_lo, y), mem: 32 (over x, z_hi, core).
Axes of the slice: x: 4, y: 4, z: 8 (z_hi: 4, z_lo: 2; z = z_hi * 2 + z_lo), core: 2. Of those that a mesh axis runs over, the one named last changes fastest.
Arguments:
- pooled: bfloat16 [32768, 5120], P(('grp', 'mem')), may hold values from -24 to 24
- grad_hidden: bfloat16 [32768, 512], P(('grp', 'mem')), may hold values from -0.059814453 to 0.059814453
- w_first: bfloat16 [5120, 512], replicated, may hold values from -0.078125 to 0.078125
- bias_first: float32 [512], replicated, may hold values from -4 to 4
- table_owner: int32 [8, 32], P('grp'), may hold values from 0 to 31, each once within a row
- shard_owner: int32 [8, 32], P('grp'), may hold values from 0 to 31, each once within a row
- lookups_whole: int32 [8, 32, 4096, 8], P('grp', 'mem'), may hold values from 0 to 1023
- lookups_split: int32 [8, 8, 4096, 8], P('grp'), may hold values from 0 to 1023
- table_whole: float32 [8, 32, 128, 1024], P('grp', 'mem'), may hold values from -3 to 3
- accum_whole: float32 [8, 32, 1024], P('grp', 'mem'), may hold values from 2e-05 to 0.0002
- table_split: float32 [8, 32, 32, 1024], P('grp', 'mem'), may hold values from -3 to 3
- accum_split: float32 [8, 8, 1024], P('grp'), may hold values from 2e-05 to 0.0002
Outputs:
- grad_first: float32 [5120, 512], P('mem')
- grad_bias: float32 [512], replicated
- new_whole: float32 [8, 32, 128, 1024], P('grp', 'mem')
- new_split: float32 [8, 32, 32, 1024], P('grp', 'mem')
Inputs may be any that keep to these rules, and one draw needn't show every extreme that they name: `table_owner`: each row is a permutation of the owner slots. `shard_owner`: each row is a permutation of the owner slots.
All inputs are finite; a program needn't handle non-finite values.
Results may differ from a plain program's by a relative error of at most 0.0055.
Values may be sent and summed in bfloat16 or wider, within the bound.
A program may use at most 128 MiB of HBM per device.

v0:
```python
import jax
import jax.numpy as jnp
from jax import lax
from jax.sharding import Mesh
from jax.sharding import PartitionSpec as P

E = 128
CS = 4
COLS = 32
MEM = ("mem_0", "mem_1", "mem_2")
GRP = ("grp_0", "grp_1")
GRP_MEM = ("grp_0", "grp_1", "mem_0", "mem_1", "mem_2")


LEARN_RATE = 0.5
EPSILON = 1e-08


def in_one_piece(arrays, axis, split_dim, concat_dim, along):
    ends, at = ([], 0)
    for a in arrays[:-1]:
        at += a.shape[along]
        ends.append(at)
    both = jnp.concatenate(arrays, axis=along)
    return tuple(
        jnp.split(
            lax.all_to_all(both, axis, split_axis=split_dim, concat_axis=concat_dim, tiled=True),
            ends,
            axis=along,
        )
    )


def copy_for_each(x, axis):
    copies = jnp.broadcast_to(x, (lax.axis_size(axis), *x.shape))
    return lax.all_to_all(copies, axis, split_axis=0, concat_axis=0, tiled=True)


def over_copies(x, axis):
    everything = copy_for_each(x, axis)
    return jnp.sum(everything, axis=0)


def one_axis_at_a_time(x, axes):
    for axis in axes:
        x = lax.psum(x, axis)
    return x


def joined_along(blocks, dim):
    dims = list(blocks.shape[1:])
    dims[dim] *= blocks.shape[0]
    return jnp.moveaxis(blocks, 0, dim).reshape(dims)


def collect(x, axis, dim):
    blocks = copy_for_each(x, axis)
    return joined_along(blocks, dim)


def tower_block(inputs, upstream, weights, bias_row):
    pre_act = jnp.dot(inputs, weights, preferred_element_type=jnp.float32) + bias_row
    sigmoid_pre = jax.nn.sigmoid(pre_act)
    gradient_slope = sigmoid_pre * (1.0 + pre_act * (1.0 - sigmoid_pre))
    delta_rows = (upstream.astype(jnp.float32) * gradient_slope).astype(jnp.bfloat16)
    back_rows = lax.dot_general(
        delta_rows, weights, (((1,), (1,)), ((), ())), preferred_element_type=jnp.float32
    ).astype(jnp.bfloat16)
    return (delta_rows, back_rows)


def arrange(back_rows, whole_order, split_order, owners):
    sample_rows = back_rows.shape[0]
    whole_part = back_rows[:, : owners * E].reshape(sample_rows, owners, E)
    split_part = back_rows[:, owners * E :].reshape(sample_rows, owners, COLS)
    return (jnp.take(whole_part, whole_order, axis=1), jnp.take(split_part, split_order, axis=1))


def row_gradient(values, key_rows, row_count):
    total_rows = values.shape[0]
    block_rows = min(512, total_rows)
    column_count = values.shape[1]
    value_blocks = values.reshape(total_rows // block_rows, block_rows, column_count)
    key_blocks = key_rows.reshape(total_rows // block_rows, block_rows, key_rows.shape[1])
    positions = lax.broadcasted_iota(jnp.int32, (1, 1, row_count), 2)

    def accumulate(running, inputs_pair):
        piece_rows, pick_keys = inputs_pair
        hit_counts = jnp.sum((pick_keys[:, :, None] == positions).astype(jnp.bfloat16), axis=1)
        added = lax.dot_general(
            piece_rows, hit_counts, (((0,), (0,)), ((), ())), preferred_element_type=jnp.float32
        )
        return (running + added, None)

    initial = jnp.zeros((column_count, row_count), jnp.float32)
    result, _ = lax.scan(accumulate, initial, (value_blocks, key_blocks))
    return result


def adagrad(weights_in, accum_rows, row_grad, squares):
    state_rows = accum_rows + squares / E
    return weights_in - LEARN_RATE * row_grad / (jnp.sqrt(state_rows) + EPSILON)


def per_device(
    pooled,
    grad_hidden,
    w_first,
    bias_first,
    table_owner,
    shard_owner,
    lookups_whole,
    lookups_split,
    table_whole,
    accum_whole,
    table_split,
    accum_split,
):
    owners = lax.axis_size(MEM)
    position = lax.axis_index(MEM)
    whole_order = jnp.argsort(table_owner[0])
    split_order = jnp.argsort(shard_owner[0])
    split_table = split_order[position] // CS
    keys_whole = lookups_whole[0, 0]
    keys_split = lax.dynamic_index_in_dim(lookups_split[0], split_table, 0, keepdims=False)
    rows_whole = table_whole.shape[-1]
    rows_split = table_split.shape[-1]
    samples = pooled.shape[0]
    delta_rows, back_rows = tower_block(pooled, grad_hidden, w_first, bias_first)
    send_whole, send_split = arrange(back_rows, whole_order, split_order, owners)
    got_whole, got_split = in_one_piece((send_whole, send_split), MEM, 1, 0, 2)
    grad_whole = row_gradient(got_whole.reshape(owners * samples, E), keys_whole, rows_whole)
    grad_split = row_gradient(got_split.reshape(owners * samples, COLS), keys_split, rows_split)
    own_rows = lax.psum_scatter(
        lax.dot_general(
            pooled, delta_rows, (((0,), (0,)), ((), ())), preferred_element_type=jnp.float32
        ),
        MEM,
        scatter_dimension=0,
        tiled=True,
    )
    grad_first = over_copies(own_rows, GRP)
    grad_bias = one_axis_at_a_time(jnp.sum(delta_rows.astype(jnp.float32), axis=0), GRP_MEM)
    new_whole = adagrad(
        table_whole[0, 0], accum_whole[0, 0], grad_whole, jnp.sum(grad_whole * grad_whole, axis=0)
    )
    shard_squares = jnp.sum(grad_split * grad_split, axis=0)
    every_shard = collect(shard_squares[None, :], MEM, 0)
    member = (split_order // CS == split_table).astype(jnp.float32)
    total_squares = jnp.dot(member, every_shard, precision=lax.Precision.HIGHEST)
    accum_here = lax.dynamic_index_in_dim(accum_split[0], split_table, 0, keepdims=False)
    new_split = adagrad(table_split[0, 0], accum_here, grad_split, total_squares)
    return (grad_first, grad_bias, new_whole[None, None], new_split[None, None])


def solution(mesh):
    finer = Mesh(mesh.devices.reshape(2, 4, 4, 4, 2), ("grp_0", "grp_1", "mem_0", "mem_1", "mem_2"))
    in_specs = (
        P(GRP_MEM, None),
        P(GRP_MEM, None),
        P(),
        P(),
        P(GRP, None),
        P(GRP, None),
        P(GRP, MEM, None, None),
        P(GRP, None, None, None),
        P(GRP, MEM, None, None),
        P(GRP, MEM, None),
        P(GRP, MEM, None, None),
        P(GRP, None, None),
    )
    out_specs = (P(MEM, None), P(), P(GRP, MEM, None, None), P(GRP, MEM, None, None))
    return jax.shard_map(
        per_device, mesh=finer, in_specs=in_specs, out_specs=out_specs, check_vma=False
    )
```

profile of v0, /device:TPU:1, one launch (start us, length us, event | category | flops | bytes accessed | tf_op | source)
XLA Modules:
  0.0 281.0 jit_solution(16323277819517830956)
XLA Ops:
  12.0 5.4 %convolution_bitcast_fusion = f32[5120,512]{0,1:T(8,128)} fusion(bf16[128,5120]{1,0:T(8,128)(2,1)S(1)} %copy-done, f32[128,512]{1,0:T(8,128)S(1)} %get-tuple-element.215, bf16[128,512]{1,0:T(8,128)(2,1)S(1)} %copy-done.3), kind=kOutput, calls=%fused_computation.20 | convolution fusion | flops 671744000 | bytes 12189696 | tf_op jit(solution)/shard_map/dot_general | solution.py:135
  17.4 11.4 %copy.48 = f32[5120,512]{1,0:T(8,128)} copy(f32[5120,512]{0,1:T(8,128)} %convolution_bitcast_fusion) | data formatting | bytes 20971520
  45.5 12.6 %all-to-all-start.1 = ((bf16[128,32,160]{0,2,1:T(8,128)(2,1)}), bf16[128,32,160]{0,2,1:T(8,128)(2,1)S(1)}, u32[]{:S(2)}, u32[]{:S(2)}) async-start(bf16[128,32,160]{0,2,1:T(8,128)(2,1)} %copy.42), calls=%async_computation.1 | async-start | bytes 2621440 | tf_op jit(solution)/shard_map/all_to_all | solution.py:27
  62.2 26.6 %all-to-all-done.1 = bf16[128,32,160]{0,2,1:T(8,128)(2,1)S(1)} async-done(((bf16[128,32,160]{0,2,1:T(8,128)(2,1)}), bf16[128,32,160]{0,2,1:T(8,128)(2,1)S(1)}, u32[]{:S(2)}, u32[]{:S(2)}) %all-to-all-start.1) | async-done | bytes 1310752 | tf_op jit(solution)/shard_map/all_to_all | solution.py:27
  91.5 54.4 %while.27 = (s32[]{:T(128)}, f32[32,1024]{1,0:T(8,128)S(1)}, bf16[8,512,32]{2,1,0:T(8,128)(2,1)}, s32[8,512,8]{1,2,0:T(8,128)S(1)}, s32[]{:T(128)}, /*index=5*/s32[]{:T(128)}) while((s32[]{:T(128)}, f32[32,1024]{1,0:T(8,128)S(1)}, bf16[8,512,32]{2,1,0:T(8,128)(2,1)}, s32[8,512,8]{1,2,0:T(8,128)S(1)}, s32[]{:T(128)}, ...), condition=%wide.region_16.17_spmd.clone, body=%wide.region_14.16_spmd.clone.sunk | while | flops 45678592 | bytes 2572383 | solution.py:96
  91.6 5.4 %fusion.59 = bf16[512,1024]{1,0:T(8,128)(2,1)S(1)} fusion(s32[512,8]{1,0:T(8,128)S(1)} %copy.62), kind=kLoop, calls=%fused_computation.14.clone.1 | loop fusion | flops 12058624 | bytes 1064960 | tf_op jit(solution)/shard_map/while/body/eval_jaxpr/reduce_sum | solution.py:89
  98.4 5.4 %fusion.59 = bf16[512,1024]{1,0:T(8,128)(2,1)S(1)} fusion(s32[512,8]{1,0:T(8,128)S(1)} %copy.62), kind=kLoop, calls=%fused_computation.14.clone.1 | loop fusion | flops 12058624 | bytes 1064960 | tf_op jit(solution)/shard_map/while/body/eval_jaxpr/reduce_sum | solution.py:89
  105.2 5.4 %fusion.59 = bf16[512,1024]{1,0:T(8,128)(2,1)S(1)} fusion(s32[512,8]{1,0:T(8,128)S(1)} %copy.62), kind=kLoop, calls=%fused_computation.14.clone.1 | loop fusion | flops 12058624 | bytes 1064960 | tf_op jit(solution)/shard_map/while/body/eval_jaxpr/reduce_sum | solution.py:89
  112.0 5.4 %fusion.59 = bf16[512,1024]{1,0:T(8,128)(2,1)S(1)} fusion(s32[512,8]{1,0:T(8,128)S(1)} %copy.62), kind=kLoop, calls=%fused_computation.14.clone.1 | loop fusion | flops 12058624 | bytes 1064960 | tf_op jit(solution)/shard_map/while/body/eval_jaxpr/reduce_sum | solution.py:89
  118.8 5.4 %fusion.59 = bf16[512,1024]{1,0:T(8,128)(2,1)S(1)} fusion(s32[512,8]{1,0:T(8,128)S(1)} %copy.62), kind=kLoop, calls=%fused_computation.14.clone.1 | loop fusion | flops 12058624 | bytes 1064960 | tf_op jit(solution)/shard_map/while/body/eval_jaxpr/reduce_sum | solution.py:89
  125.6 5.4 %fusion.59 = bf16[512,1024]{1,0:T(8,128)(2,1)S(1)} fusion(s32[512,8]{1,0:T(8,128)S(1)} %copy.62), kind=kLoop, calls=%fused_computation.14.clone.1 | loop fusion | flops 12058624 | bytes 1064960 | tf_op jit(solution)/shard_map/while/body/eval_jaxpr/reduce_sum | solution.py:89
  132.4 5.4 %fusion.59 = bf16[512,1024]{1,0:T(8,128)(2,1)S(1)} fusion(s32[512,8]{1,0:T(8,128)S(1)} %copy.62), kind=kLoop, calls=%fused_computation.14.clone.1 | loop fusion | flops 12058624 | bytes 1064960 | tf_op jit(solution)/shard_map/while/body/eval_jaxpr/reduce_sum | solution.py:89
  139.2 5.4 %fusion.59 = bf16[512,1024]{1,0:T(8,128)(2,1)S(1)} fusion(s32[512,8]{1,0:T(8,128)S(1)} %copy.62), kind=kLoop, calls=%fused_computation.14.clone.1 | loop fusion | flops 12058624 | bytes 1064960 | tf_op jit(solution)/shard_map/while/body/eval_jaxpr/reduce_sum | solution.py:89
  146.6 7.8 %all-to-all-start.2 = ((f32[32,1,1024]{2,1,0:T(1,128)}), f32[32,1,1024]{2,1,0:T(1,128)S(1)}, u32[]{:S(2)}, u32[]{:S(2)}) async-start(f32[32,1,1024]{2,1,0:T(1,128)} %broadcast_in_dim.58), calls=%async_computation.2 | async-start | bytes 262144 | tf_op jit(solution)/shard_map/all_to_all | solution.py:36
  154.5 9.1 %psum.35 = f32[512]{0:T(512)S(1)} all-reduce(f32[512]{0:T(512)S(1)} %get-tuple-element.214), channel_id=1, replica_groups=mesh['grp_0'=2,'grp_1'=4,'mem_0'=4,'mem_1'=4,'mem_2'=2] {'grp_0'}, use_global_device_ids=true, to_apply=%region_3.4 | all-reduce | flops 512 | bytes 4096 | tf_op jit(solution)/shard_map/psum | solution.py:46
  163.6 8.4 %psum.36 = f32[512]{0:T(512)S(1)} all-reduce(f32[512]{0:T(512)S(1)} %psum.35), channel_id=1, replica_groups=mesh['grp_0'=2,'grp_1'=4,'mem_0'=4,'mem_1'=4,'mem_2'=2] {'grp_1'}, use_global_device_ids=true, to_apply=%region_4.5 | all-reduce | flops 512 | bytes 4096 | tf_op jit(solution)/shard_map/psum | solution.py:46
  172.0 8.9 %psum.37 = f32[512]{0:T(512)S(1)} all-reduce(f32[512]{0:T(512)S(1)} %psum.36), channel_id=1, replica_groups=mesh['grp_0'=2,'grp_1'=4,'mem_0'=4,'mem_1'=4,'mem_2'=2] {'mem_0'}, use_global_device_ids=true, to_apply=%region_5.6 | all-reduce | flops 512 | bytes 4096 | tf_op jit(solution)/shard_map/psum | solution.py:46
  180.8 8.3 %psum.38 = f32[512]{0:T(512)S(1)} all-reduce(f32[512]{0:T(512)S(1)} %psum.37), channel_id=1, replica_groups=mesh['grp_0'=2,'grp_1'=4,'mem_0'=4,'mem_1'=4,'mem_2'=2] {'mem_1'}, use_global_device_ids=true, to_apply=%region_6.7 | all-reduce | flops 512 | bytes 4096 | tf_op jit(solution)/shard_map/psum | solution.py:46
  189.1 9.4 %psum.39 = f32[512]{0:T(512)} all-reduce(f32[512]{0:T(512)S(1)} %psum.38), channel_id=1, replica_groups=mesh['grp_0'=2,'grp_1'=4,'mem_0'=4,'mem_1'=4,'mem_2'=2] {'mem_2'}, use_global_device_ids=true, to_apply=%region_7.8 | all-reduce | flops 512 | bytes 4096 | tf_op jit(solution)/shard_map/psum | solution.py:46
  208.0 60.5 %while.26 = (s32[]{:T(128)}, f32[128,1024]{1,0:T(8,128)S(1)}, bf16[8,512,128]{2,1,0:T(8,128)(2,1)}, s32[8,512,8]{1,2,0:T(8,128)}, s32[]{:T(128)}, /*index=5*/s32[]{:T(128)}) while((s32[]{:T(128)}, f32[128,1024]{1,0:T(8,128)S(1)}, bf16[8,512,128]{2,1,0:T(8,128)(2,1)}, s32[8,512,8]{1,2,0:T(8,128)}, s32[]{:T(128)}, ...), condition=%wide.region_12.13_spmd.clone, body=%wide.region_10.12_spmd.clone.sunk | while | flops 146538496 | bytes 3358815 | solution.py:96
  208.9 5.4 %fusion.56 = bf16[512,1024]{1,0:T(8,128)(2,1)S(1)} fusion(s32[512,8]{1,0:T(8,128)S(1)} %copy.61), kind=kLoop, calls=%fused_computation.6.clone.1 | loop fusion | flops 12058624 | bytes 1064960 | tf_op jit(solution)/shard_map/while/body/eval_jaxpr/reduce_sum | solution.py:89
  216.5 5.4 %fusion.56 = bf16[512,1024]{1,0:T(8,128)(2,1)S(1)} fusion(s32[512,8]{1,0:T(8,128)S(1)} %copy.61), kind=kLoop, calls=%fused_computation.6.clone.1 | loop fusion | flops 12058624 | bytes 1064960 | tf_op jit(solution)/shard_map/while/body/eval_jaxpr/reduce_sum | solution.py:89
  224.0 5.4 %fusion.56 = bf16[512,1024]{1,0:T(8,128)(2,1)S(1)} fusion(s32[512,8]{1,0:T(8,128)S(1)} %copy.61), kind=kLoop, calls=%fused_computation.6.clone.1 | loop fusion | flops 12058624 | bytes 1064960 | tf_op jit(solution)/shard_map/while/body/eval_jaxpr/reduce_sum | solution.py:89
  231.6 5.4 %fusion.56 = bf16[512,1024]{1,0:T(8,128)(2,1)S(1)} fusion(s32[512,8]{1,0:T(8,128)S(1)} %copy.61), kind=kLoop, calls=%fused_computation.6.clone.1 | loop fusion | flops 12058624 | bytes 1064960 | tf_op jit(solution)/shard_map/while/body/eval_jaxpr/reduce_sum | solution.py:89
  (115 shorter events, 90.7 us)
Async XLA Ops:
  7.2 1.3 copy-start
  7.2 4.8 %copy-start.3 = (bf16[128,512]{1,0:T(8,128)(2,1)S(1)}, bf16[128,512]{1,0:T(8,128)(2,1)}, u32[]{:S(2)}) copy-start(bf16[128,512]{1,0:T(8,128)(2,1)} %param.17) | copy-start | bytes 393220
  7.2 193.4 %reduce-scatter.4.cloned.1.call-start = ((), (), s32[]{:S(2)}) async-start(), calls=%async_computation.4 | async-start | bytes 10813440 | tf_op jit(solution)/shard_map/reduce_scatter | solution.py:134
  28.9 4.5 %copy-start.6 = (s32[1,32]{1,0:T(1,128)S(1)}, s32[1,32]{1,0:T(1,128)}, u32[]{:S(2)}) copy-start(s32[1,32]{1,0:T(1,128)} %param.20) | copy-start | bytes 388
  28.9 6.1 %copy-start.7 = (s32[1,32]{1,0:T(1,128)S(1)}, s32[1,32]{1,0:T(1,128)}, u32[]{:S(2)}) copy-start(s32[1,32]{1,0:T(1,128)} %param.21) | copy-start | bytes 388
  39.8 2.1 copy-start.2
  45.5 43.4 %all-to-all-start.1 = ((bf16[128,32,160]{0,2,1:T(8,128)(2,1)}), bf16[128,32,160]{0,2,1:T(8,128)(2,1)S(1)}, u32[]{:S(2)}, u32[]{:S(2)}) async-start(bf16[128,32,160]{0,2,1:T(8,128)(2,1)} %copy.42), calls=%async_computation.1 | async-start | bytes 2621440 | tf_op jit(solution)/shard_map/all_to_all | solution.py:27
  89.0 1.1 copy-start.1
  145.8 53.4 %slice-start = ((bf16[4096,1,160]{0,2,1:T(8,128)(2,1)}), bf16[4096,1,128]{0,2,1:T(8,128)(2,1)S(1)}, s32[]{:S(2)}) async-start(bf16[4096,1,160]{0,2,1:T(8,128)(2,1)} %copy-done.1), calls=%async_computation.5 | async-start | bytes 2097152 | tf_op jit(solution)/shard_map/split | solution.py:26
  146.6 54.0 %all-to-all-start.2 = ((f32[32,1,1024]{2,1,0:T(1,128)}), f32[32,1,1024]{2,1,0:T(1,128)S(1)}, u32[]{:S(2)}, u32[]{:S(2)}) async-start(f32[32,1,1024]{2,1,0:T(1,128)} %broadcast_in_dim.58), calls=%async_computation.2 | async-start | bytes 262144 | tf_op jit(solution)/shard_map/all_to_all | solution.py:36
  203.4 68.0 %all-to-all-start = ((f32[8,160,512]{2,1,0:T(8,128)}), f32[8,160,512]{2,1,0:T(8,128)}, u32[]{:S(2)}, u32[]{:S(2)}) async-start(f32[8,160,512]{2,1,0:T(8,128)} %broadcast_in_dim.48), calls=%async_computation | async-start | bytes 5242880 | tf_op jit(solution)/shard_map/all_to_all | solution.py:36
  208.0 60.6 %copy-start.5 = (f32[1,1,1024]{2,1,0:T(1,128)S(1)}, f32[1,1,1024]{2,1,0:T(1,128)}, u32[]{:S(2)}) copy-start(f32[1,1,1024]{2,1,0:T(1,128)} %param.25) | copy-start | bytes 12292
  208.0 62.7 %copy-start.4 = (f32[1,1,32,1024]{3,2,1,0:T(8,128)S(1)}, f32[1,1,32,1024]{3,2,1,0:T(8,128)}, u32[]{:S(2)}) copy-start(f32[1,1,32,1024]{3,2,1,0:T(8,128)} %param.26) | copy-start | bytes 393220
Sparse Core Ops, SparseCore 0:
  29.0 133.6 reduce-scatter.3
where the time goes:
time: 283 us; the launch traced here: 281 us
  other arithmetic  95.8 us (34%)
  blocking collectives  44 us (16%)
  local copies, waits for them, and re-layouts  38.4 us (14%)
  matrix products  33.4 us (12%)
  waiting for transfers between devices  26.6 us (9%)
  starting transfers between devices  25 us (9%)
  between operations  17 us (6%)
    reduce_sum x16, other arithmetic, accumulate(): jnp.sum((pick_keys[:, :, None] == positions).astype(jnp.bfloat16), axis=1)  86.3 us
    psum x5, blocking collectives, one_axis_at_a_time(): x = lax.psum(x, axis)  44 us
    all_to_all x1, waiting for transfers between devices, in_one_piece(): lax.all_to_all(both, axis, split_axis=split_dim, concat_axis=concat_dim,...  26.6 us
    dot_general x16, matrix products, accumulate(): lax.dot_general(piece_rows, hit_counts, (((0,), (0,)), ((), ())), preferr...  20 us
    unnamed x19, local copies, waits for them, and re-layouts  16.4 us
    all_to_all x1, starting transfers between devices, in_one_piece(): lax.all_to_all(both, axis, split_axis=split_dim, concat_axis=concat_dim,...  12.6 us
    all_to_all x2, starting transfers between devices, copy_for_each(): return lax.all_to_all(copies, axis, split_axis=0, concat_axis=0, tiled=True)  12.4 us
    eq x32, local copies, waits for them, and re-layouts, accumulate(): pick_keys[:, :, None] == positions  7.84 us
  transfers between devices with their start and end apart: 4, of which 1 were waited for; matrix products, arithmetic and copies ran while one was open for 50% of the time, Pallas kernels for 0%

commit v1 on v0

v1 whole, which is shorter than its diff:
```python
import jax
import jax.numpy as jnp
from jax import lax
from jax.experimental import pallas as pl
from jax.experimental.pallas import tpu as pltpu
from jax.sharding import Mesh
from jax.sharding import PartitionSpec as P

E = 128
CS = 4
COLS = 32
ZL, Y, X, ZH, C = "grp_0", "grp_1", "mem_0", "mem_1", "mem_2"
SIZE = {ZL: 2, Y: 4, X: 4, ZH: 4, C: 2}
MEM = (X, ZH, C)
GRP = (ZL, Y)
GRP_MEM = GRP + MEM
LEARN_RATE = 0.5
EPSILON = 1e-08
MESH = pl.DeviceIdType.MESH
BF = jnp.bfloat16
F32 = jnp.float32


def remote(src, dst, ssem, rsem, dev):
    return pltpu.make_async_remote_copy(
        src_ref=src, dst_ref=dst, send_sem=ssem, recv_sem=rsem, device_id=dev, device_id_type=MESH
    )


def kernel(
    owner_ref, sowner_ref, pooled_ref, gh_ref, w_hbm, bias_ref, lkw_ref, lks_ref,
    tw_ref, aw_ref, ts_ref, as_ref,
    gf_ref, gb_ref, nw_ref, ns_ref,
    w_v, pt, pr, gbuf, pp, yr, zs, zr, bs, br, cw, cs, accw, accs, bacc, wtct, pre, keys_c, gr,
    w_sem, own_sem, sp, rp, sa, sb, sc, rg, sy, ry, sz, rz, sg, rgf, sbi, rbi,
):
    x, zh, c = lax.axis_index(X), lax.axis_index(ZH), lax.axis_index(C)
    y, zl = lax.axis_index(Y), lax.axis_index(ZL)

    def off(axis, d):
        return lax.rem(lax.axis_index(axis) + d, SIZE[axis])

    load_w = pltpu.make_async_copy(w_hbm, w_v, w_sem)
    load_w.start()

    barrier = pltpu.get_barrier_semaphore()
    peers = []
    for d in (1, 2, 3):
        peers.append({X: off(X, d)})
        peers.append({X: off(X, d), C: 1 - c})
        peers.append({ZH: off(ZH, d)})
        peers.append({ZH: off(ZH, d), ZL: 1 - zl})
        peers.append({Y: off(Y, d)})
        peers.append({Y: off(Y, d), ZL: 1 - zl})
    peers.append({C: 1 - c})
    peers.append({ZL: 1 - zl})
    for p in peers:
        pl.semaphore_signal(barrier, inc=1, device_id=p, device_id_type=MESH)
    pl.semaphore_wait(barrier, len(peers))

    for t in range(40):
        tile = pooled_ref[:, 128 * t : 128 * t + 128].T
        done = 0
        while done < 128:
            f = 128 * t + done
            m, r = f // 160, f % 160
            n = min(160 - r, 128 - done)
            pt[(m // 8), m % 2, (m // 2) % 4, r : r + n, :] = tile[done : done + n, :]
            done += n

    def piece(dx, dc):
        xd, cd = off(X, dx), off(C, dc)
        i = dx * 2 + dc
        return remote(pt.at[xd, cd], pr.at[x * 2 + c], sp.at[i], rp.at[x * 2 + c], {X: xd, C: cd})

    def piece_in(xs, csrc):
        return remote(pt.at[0, 0], pr.at[xs * 2 + csrc], sp.at[0], rp.at[xs * 2 + csrc], {C: 1 - c})

    own_piece = pltpu.make_async_copy(pt.at[x, c], pr.at[x * 2 + c], own_sem)
    own_piece.start()
    piece(0, 1).start()
    piece(1, 0).start()
    piece(3, 0).start()

    load_w.wait()
    pre[...] = jnp.zeros_like(pre)

    @pl.loop(0, 8)
    def _(k):
        cols = pl.ds(pl.multiple_of(k * 640, 640), 640)
        wk = w_v[pl.ds(k * 5, 5)].reshape(640, 512)
        pre[...] += jnp.dot(pooled_ref[:, cols], wk, preferred_element_type=F32)

    pre_act = pre[...] + bias_ref[...]
    sg_ = jax.nn.sigmoid(pre_act)
    slope = sg_ * (1.0 + pre_act * (1.0 - sg_))
    my_rows = pl.ds(pl.multiple_of(c * 128, 128), 128)
    gbuf[x * 4 + zh, my_rows, :] = (gh_ref[...].astype(F32) * slope).astype(BF)

    def half(h, a, b, cc):
        rows = pl.ds(pl.multiple_of(cc * 128 + h * 64, 64), 64)
        return gbuf.at[a * 4 + b, rows, :]

    def slot(h, a, b, cc):
        return rg.at[h, a * 8 + b * 2 + cc]

    def first_hop(h, d):
        ref = half(h, x, zh, c)
        dev = {ZH: off(ZH, d)} if h == 0 else {X: off(X, d)}
        return remote(ref, ref, sa.at[h, d - 1], slot(h, x, zh, c), dev)

    def second_hop(h, e, d):
        a, b = (x, off(ZH, e)) if h == 0 else (off(X, e), zh)
        ref = half(h, a, b, c)
        dev = {X: off(X, d)} if h == 0 else {ZH: off(ZH, d)}
        return remote(ref, ref, sb.at[h, e * 3 + d - 1], slot(h, a, b, c), dev)

    def to_core(h, da, db):
        a, b = off(X, da), off(ZH, db)
        ref = half(h, a, b, c)
        return remote(ref, ref, sc.at[h, da * 4 + db], slot(h, a, b, c), {C: 1 - c})

    def arrive(h, da, db, dc):
        a, b, cc = off(X, da), off(ZH, db), off(C, dc)
        ref = half(h, a, b, cc)
        remote(ref, ref, sa.at[0, 0], slot(h, a, b, cc), {C: 1 - c}).wait_recv()

    for h in (1, 0):
        for d in (1, 3, 2):
            first_hop(h, d).start()
    for h in (0, 1):
        for d in (1, 3, 2):
            second_hop(h, 0, d).start()
    for h in (0, 1):
        to_core(h, 0, 0).start()
    piece(1, 1).start()
    piece(3, 1).start()
    piece(2, 0).start()
    piece(2, 1).start()

    me = x * 8 + zh * 2 + c

    def find(ref, label):
        return lax.fori_loop(0, 32, lambda i, at: jnp.where(ref[0, i] == me, label(i), at), 0)

    whole_t = find(owner_ref, lambda i: i)
    split_t = find(sowner_ref, lambda i: 32 + i // CS)
    split_c = find(sowner_ref, lambda i: i // CS)
    quarter = find(sowner_ref, lambda i: lax.rem(i, CS))
    wtct[:, :128] = w_v[whole_t].T
    wtct[:, 128:] = w_v[split_t].T
    keys_c[...] = lks_ref[split_c]

    def count_block(keys, out, cols):
        lo = jnp.bitwise_and(keys, 127)
        field = jnp.left_shift(1, jnp.right_shift(keys, 7) * 4)
        sub = lax.broadcasted_iota(jnp.int32, (128, 128), 0)
        packed = jnp.zeros((128, 128), jnp.int32)
        for p in range(8):
            packed += jnp.where(lo[p : p + 1, :] == sub, field[p : p + 1, :], 0)
        for h in range(8):
            n = jnp.bitwise_and(jnp.right_shift(packed, 4 * h), 15)
            out[h * 128 : h * 128 + 128, cols] = n.astype(F32).astype(BF)

    def count(k, carry=None):
        cols = pl.ds(pl.multiple_of(k * 128, 128), 128)
        count_block(lkw_ref[:, cols], cw, cols)
        count_block(keys_c[:, cols], cs, cols)

    @pl.loop(0, 3)
    def _(j):
        e = 1 + lax.rem(2 * j, 3)
        for h in (1, 0):
            da, db = (0, e) if h == 0 else (e, 0)
            pl.loop(j * 10 + (1 - h) * 5, j * 10 + (1 - h) * 5 + 5)(lambda k: count(k))
            arrive(h, da, db, 0)
            for d in (1, 3, 2):
                second_hop(h, e, d).start()
            to_core(h, da, db).start()

    pl.loop(30, 32)(lambda k: count(k))

    for d in (1, 3, 2):
        arrive(0, d, 0, 0)
        to_core(0, d, 0).start()
    own_piece.wait()
    for i in range(1, 8):
        piece_in(off(X, i // 2), off(C, i % 2)).wait_recv()
    for d in range(4):
        for h in (0, 1):
            arrive(h, d, 0, 1)

    @pl.loop(0, 4)
    def _(q):
        total = jnp.zeros((160, 512), F32)
        for xs in range(4):
            both = jnp.concatenate([pr[2 * xs, q], pr[2 * xs + 1, q]], axis=1)
            total += jnp.dot(both, gbuf[xs * 4 + zh], preferred_element_type=F32)
        low = total.astype(BF)
        for j in range(4):
            pp[j, q] = low[:, 128 * j : 128 * j + 128]

    def along_y(d):
        yd = off(Y, d)
        return remote(pp.at[yd], yr.at[y], sy.at[d - 1], ry.at[y], {Y: yd})

    def from_y(d):
        ys = off(Y, d)
        return remote(pp.at[ys], yr.at[ys], sy.at[0], ry.at[ys], {Y: ys})

    for d in (1, 3, 2):
        along_y(d).start()

    accw[...] = jnp.zeros_like(accw)
    accs[...] = jnp.zeros_like(accs)
    bacc[...] = jnp.zeros_like(bacc)

    def tables(da, db):
        cb = off(X, da) * 4 + off(ZH, db)
        rows = gbuf[cb]
        cols = pl.ds(pl.multiple_of(cb * 256, 256), 256)
        back = jnp.dot(rows, wtct[...], preferred_element_type=F32).astype(BF)
        accw[...] += jnp.dot(cw[:, cols], back[:, :128], preferred_element_type=F32)
        accs[...] += jnp.dot(cs[:, cols], back[:, 128:], preferred_element_type=F32)
        bacc[...] += jnp.dot(jnp.ones((8, 256), BF), rows, preferred_element_type=F32)

    tables(0, 0)

    for b in (1, 3, 2):
        arrive(1, 0, b, 0)
        to_core(1, 0, b).start()
        tables(b, 0)

    for d in (1, 3, 2):
        from_y(d).wait_recv()

    @pl.loop(0, 4)
    def _(q):
        total = pp[y, q].astype(F32)
        for d in (1, 2, 3):
            total += yr[off(Y, d), q].astype(F32)
        zs[q * 2] = total[:80].astype(BF)
        zs[q * 2 + 1] = total[80:].astype(BF)

    zme = zh * 2 + zl
    others = [(1, 0), (3, 0), (0, 1), (1, 1), (3, 1), (2, 0), (2, 1)]

    def along_z(i):
        zd, ld = off(ZH, others[i][0]), off(ZL, others[i][1])
        return remote(zs.at[zd * 2 + ld], zr.at[zme], sz.at[i], rz.at[zme], {ZH: zd, ZL: ld})

    def from_z(i):
        s = off(ZH, others[i][0]) * 2 + off(ZL, others[i][1])
        return remote(zs.at[s], zr.at[s], sz.at[0], rz.at[s], {C: 1 - c})

    for i in range(7):
        along_z(i).start()

    for b in (1, 3, 2):
        arrive(0, 0, b, 1)
        arrive(1, 0, b, 1)
        tables(0, b)

    def far(k):
        return (1, 3, 2)[k // 3], (1, 3, 2)[k % 3]

    def relay(k):
        da, db = far(k)
        for h in (0, 1):
            arrive(h, da, db, 0)
            to_core(h, da, db).start()

    def far_tables(k):
        da, db = far(k)
        arrive(0, da, db, 1)
        arrive(1, da, db, 1)
        tables(da, db)

    relay(0)

    for k in range(4):
        relay(k + 1)
        far_tables(k)

    for i in range(7):
        from_z(i).wait_recv()
    total = zs[zme].astype(F32)
    for i in range(7):
        total += zr[off(ZH, others[i][0]) * 2 + off(ZL, others[i][1])].astype(F32)

    gme = y * 2 + zl
    gr[gme] = total
    group = [(1, 0), (3, 0), (0, 1), (1, 1), (3, 1), (2, 0), (2, 1)]

    def give(i):
        yd, ld = off(Y, group[i][0]), off(ZL, group[i][1])
        return remote(gr.at[gme], gr.at[gme], sg.at[i], rgf.at[gme], {Y: yd, ZL: ld})

    def take(i):
        g = off(Y, group[i][0]) * 2 + off(ZL, group[i][1])
        return remote(gr.at[g], gr.at[g], sg.at[0], rgf.at[g], {C: 1 - c})

    for i in range(7):
        give(i).start()

    for k in range(4, 8):
        relay(k + 1)
        far_tables(k)

    far_tables(8)

    bs[...] = bacc[...]

    def give_bias(i):
        yd, ld = off(Y, group[i][0]), off(ZL, group[i][1])
        return remote(bs, br.at[y * 2 + zl], sbi.at[i], rbi.at[y * 2 + zl], {Y: yd, ZL: ld})

    def take_bias(i):
        s = off(Y, group[i][0]) * 2 + off(ZL, group[i][1])
        return remote(bs, br.at[s], sbi.at[0], rbi.at[s], {C: 1 - c})

    for i in range(7):
        give_bias(i).start()

    grad = accw[...].T
    square = jnp.sum(grad * grad, axis=0, keepdims=True)
    scale = LEARN_RATE / (jnp.sqrt(aw_ref[...] + square / E) + EPSILON)
    nw_ref[...] = tw_ref[...] - grad * scale
    grads = accs[...].T
    squares = jnp.sum(grads * grads, axis=0, keepdims=True)
    tab = lax.broadcasted_iota(jnp.int32, (8, 1024), 0)
    state = jnp.sum(jnp.where(tab == split_c, as_ref[...], 0.0), axis=0, keepdims=True)
    scales = LEARN_RATE / (jnp.sqrt(state + squares / E) + EPSILON)
    mine = grads[:COLS]
    for q in range(1, CS):
        mine = jnp.where(quarter == q, grads[q * COLS : (q + 1) * COLS], mine)
    ns_ref[...] = ts_ref[...] - mine * scales

    for i in range(7):
        take_bias(i).wait_recv()
    bias_sum = bs[0:1, :]
    for i in range(7):
        s = off(Y, group[i][0]) * 2 + off(ZL, group[i][1])
        bias_sum += br[s, 0:1, :]
    gb_ref[...] = bias_sum

    for i in range(7):
        take(i).wait_recv()
    for yy in range(4):
        for ll in range(2):
            gf_ref[80 * ll : 80 * ll + 80, 128 * yy : 128 * yy + 128] = gr[yy * 2 + ll]
    for i in range(1, 8):
        piece(i // 2, i % 2).wait_send()
    for h in (0, 1):
        for d in (1, 2, 3):
            first_hop(h, d).wait_send()

        @pl.loop(0, 4)
        def _(e):
            for d in (1, 2, 3):
                second_hop(h, e, d).wait_send()

        @pl.loop(0, 16)
        def _(i):
            to_core(h, i // 4, lax.rem(i, 4)).wait_send()

    for d in (1, 2, 3):
        along_y(d).wait_send()
    for i in range(7):
        along_z(i).wait_send()
        give(i).wait_send()
        give_bias(i).wait_send()


VM = pl.BlockSpec(memory_space=pltpu.VMEM)
SM = pl.BlockSpec(memory_space=pltpu.SMEM)
ANY = pl.BlockSpec(memory_space=pl.ANY)
DMA = pltpu.SemaphoreType.DMA


def per_device(
    pooled, grad_hidden, w_first, bias_first, table_owner, shard_owner, lookups_whole,
    lookups_split, table_whole, accum_whole, table_split, accum_split,
):
    keys_whole = jnp.swapaxes(lookups_whole[0, 0], 0, 1)
    keys_split = jnp.swapaxes(lookups_split[0], 1, 2)
    outs = pl.pallas_call(
        kernel,
        out_shape=(
            jax.ShapeDtypeStruct((160, 512), F32),
            jax.ShapeDtypeStruct((1, 512), F32),
            jax.ShapeDtypeStruct((128, 1024), F32),
            jax.ShapeDtypeStruct((32, 1024), F32),
        ),
        in_specs=[SM, SM, VM, VM, ANY, VM, VM, VM, VM, VM, VM, VM],
        out_specs=(VM, VM, VM, VM),
        scratch_shapes=[
            pltpu.VMEM((40, 128, 512), BF),
            pltpu.VMEM((4, 2, 4, 160, 128), BF),
            pltpu.VMEM((8, 4, 160, 128), BF),
            pltpu.VMEM((16, 256, 512), BF),
            pltpu.VMEM((4, 4, 160, 128), BF),
            pltpu.VMEM((4, 4, 160, 128), BF),
            pltpu.VMEM((8, 80, 128), BF),
            pltpu.VMEM((8, 80, 128), BF),
            pltpu.VMEM((8, 512), F32),
            pltpu.VMEM((8, 8, 512), F32),
            pltpu.VMEM((1024, 4096), BF),
            pltpu.VMEM((1024, 4096), BF),
            pltpu.VMEM((1024, 128), F32),
            pltpu.VMEM((1024, 128), F32),
            pltpu.VMEM((8, 512), F32),
            pltpu.VMEM((512, 256), BF),
            pltpu.VMEM((128, 512), F32),
            pltpu.VMEM((8, 4096), jnp.int32),
            pltpu.VMEM((8, 80, 128), F32),
            DMA,
            DMA,
            DMA((8,)), DMA((8,)),
            DMA((2, 3)), DMA((2, 12)), DMA((2, 16)), DMA((2, 32)),
            DMA((3,)), DMA((4,)),
            DMA((7,)), DMA((8,)),
            DMA((7,)), DMA((8,)),
            DMA((7,)), DMA((8,)),
        ],
        compiler_params=pltpu.CompilerParams(
            collective_id=0, has_side_effects=True, vmem_limit_bytes=58 * 2**20
        ),
        name="step",
    )(
        table_owner, shard_owner, pooled, grad_hidden, w_first.reshape(40, 128, 512), bias_first[None], keys_whole,
        keys_split, table_whole[0, 0], accum_whole[0], table_split[0, 0], accum_split[0],
    )
    grad_first, grad_bias, new_whole, new_split = outs
    return grad_first, grad_bias[0], new_whole[None, None], new_split[None, None]


def solution(mesh):
    finer = Mesh(mesh.devices.reshape(2, 4, 4, 4, 2), GRP_MEM)
    in_specs = (
        P(GRP_MEM, None),
        P(GRP_MEM, None),
        P(),
        P(),
        P(GRP, None),
        P(GRP, None),
        P(GRP, MEM, None, None),
        P(GRP, None, None, None),
        P(GRP, MEM, None, None),
        P(GRP, MEM, None),
        P(GRP, MEM, None, None),
        P(GRP, None, None),
    )
    out_specs = (P(MEM, None), P(), P(GRP, MEM, None, None), P(GRP, MEM, None, None))
    return jax.shard_map(
        per_device, mesh=finer, in_specs=in_specs, out_specs=out_specs, check_vma=False
    )
```

time: 283 us -> 70.5 us (0.25)
  other arithmetic: 95.8 us -> 0 us
  Pallas kernels: 0 us -> 63.2 us
  blocking collectives: 44 us -> 0 us
  matrix products: 33.4 us -> 0 us
  local copies, waits for them, and re-layouts: 38.4 us -> 6.42 us
  waiting for transfers between devices: 26.6 us -> 0 us
  starting transfers between devices: 25 us -> 0 us
  between operations: 17 us -> 0.65 us
    reduce_sum x19 -> x0, other arithmetic: 89.1 us -> none  [the longest x16 86.3 us: accumulate(): jnp.sum((pick_keys[:, :, None] == positions).astype(jnp.bfloat16), axis=1)]
    pallas_call x0 -> x1, Pallas kernels: none -> 63.2 us  [per_device(): pl.pallas_call(kernel, out_shape=(jax.ShapeDtypeStruct((160, 512), F32),...]
    psum x5 -> x0, blocking collectives: 44 us -> none  [one_axis_at_a_time(): x = lax.psum(x, axis)]
    dot_general x20 -> x0, matrix products: 33.4 us -> none  [the longest x16 20 us: accumulate(): lax.dot_general(piece_rows, hit_counts, (((0,), (0,)), ((), ())), preferr...]
    all_to_all x3 -> x0, waiting for transfers between devices: 26.6 us -> none  [the longest x1 26.6 us: in_one_piece(): lax.all_to_all(both, axis, split_axis=split_dim, concat_axis=concat_dim,...]
    all_to_all x3 -> x0, starting transfers between devices: 25 us -> none  [the longest x1 12.6 us: in_one_piece(): lax.all_to_all(both, axis, split_axis=split_dim, concat_axis=concat_dim,...]
    unnamed x19 -> x4, local copies, waits for them, and re-layouts: 16.4 us -> 6.42 us
    eq x32 -> x0, local copies, waits for them, and re-layouts: 7.84 us -> none  [accumulate(): pick_keys[:, :, None] == positions]
  transfers between devices with their start and end apart: 4 -> 0, of which waited for: 1 -> 0; matrix products, arithmetic and copies ran while one was open for 50% -> 0% of each run, Pallas kernels for 0% -> 0%
where the time goes in v1:
time: 70.5 us; the launch traced here: 70.3 us
  Pallas kernels  63.2 us (90%)
  local copies, waits for them, and re-layouts  6.42 us (9%)
    pallas_call x1, Pallas kernels, per_device(): pl.pallas_call(kernel, out_shape=(jax.ShapeDtypeStruct((160, 512), F32),...  63.2 us
    unnamed x4, local copies, waits for them, and re-layouts  6.42 us

profile of v1, /device:TPU:1, one launch (start us, length us, event | category | flops | bytes accessed | tf_op | source)
XLA Modules:
  0.0 70.3 jit_solution(12143331045778189261)
XLA Ops:
  0.6 63.2 %step.1 = (f32[160,512]{1,0:T(8,128)}, f32[1,512]{1,0:T(1,128)}, f32[128,1024]{1,0:T(8,128)}, f32[32,1024]{1,0:T(8,128)}) custom-call(s32[1,32]{1,0:T(1,128)} %owner_ref.1, s32[1,32]{1,0:T(1,128)} %sowner_ref.1, bf16[128,5120]{1,0:T(8,128)(2,1)} %pooled_ref.1, bf16[128,512]{1,0:T(8,128)(2,1)} %gh_ref.1, bf16[40,128,512]{2,1,0:T(8,128)(2,1)} %bitcast.15, ...), custom_call_target="tpu_custom_call" | custom-call | tf_op jit(solution)/shard_map/step/pallas_call | solution.py:387
  63.9 1.7 %copy.20 = f32[160,512]{1,0:T(8,128)} copy(f32[160,512]{1,0:T(8,128)} %get-tuple-element.16) | data formatting | bytes 655360
  65.6 1.3 %copy.21 = f32[512]{0:T(512)} copy(f32[512]{0:T(512)} %bitcast.25) | data formatting | bytes 4096
  66.8 1.9 %copy.22 = f32[1,1,128,1024]{3,2,1,0:T(8,128)} copy(f32[1,1,128,1024]{3,2,1,0:T(8,128)} %bitcast.18) | data formatting | bytes 1048576
  68.7 1.6 %copy.23 = f32[1,1,32,1024]{3,2,1,0:T(8,128)} copy(f32[1,1,32,1024]{3,2,1,0:T(8,128)} %bitcast.21) | data formatting | bytes 262144

commit v2 on v1

v2 whole, which is shorter than its diff:
```python
import jax
import jax.numpy as jnp
from jax import lax
from jax.experimental import pallas as pl
from jax.experimental.pallas import tpu as pltpu
from jax.sharding import Mesh
from jax.sharding import PartitionSpec as P

E = 128
CS = 4
COLS = 32
ZL, Y, X, ZH, C = "grp_0", "grp_1", "mem_0", "mem_1", "mem_2"
SIZE = {ZL: 2, Y: 4, X: 4, ZH: 4, C: 2}
MEM = (X, ZH, C)
GRP = (ZL, Y)
GRP_MEM = GRP + MEM
LEARN_RATE = 0.5
EPSILON = 1e-08
MESH = pl.DeviceIdType.MESH
BF = jnp.bfloat16
F32 = jnp.float32


def remote(src, dst, ssem, rsem, dev):
    return pltpu.make_async_remote_copy(
        src_ref=src, dst_ref=dst, send_sem=ssem, recv_sem=rsem, device_id=dev, device_id_type=MESH
    )


def kernel(
    owner_ref, sowner_ref, pooled_ref, gh_ref, w_hbm, bias_ref, lkw_ref, lks_hbm,
    gf_ref, gb_ref, accw, accs,
    w_v, lks_ref, pt, pr, gbuf, pp, yr, zs, zr, bs, by, bt, bz, cw, cs, wtct, pre, keys_c, gr,
    w_sem, lk_sem, own_sem, sp, rp, sa, sb, sc, rg, rh, sy, ry, sz, rz, sg, rgf, sby, rby, sbz, rbz,
):
    x, zh, c = lax.axis_index(X), lax.axis_index(ZH), lax.axis_index(C)
    y, zl = lax.axis_index(Y), lax.axis_index(ZL)

    def off(axis, d):
        return lax.rem(lax.axis_index(axis) + d, SIZE[axis])

    load_w = pltpu.make_async_copy(w_hbm, w_v, w_sem)
    load_w.start()
    load_keys = pltpu.make_async_copy(lks_hbm, lks_ref, lk_sem)
    load_keys.start()

    barrier = pltpu.get_barrier_semaphore()
    peers = []
    for d in (1, 2, 3):
        peers.append({X: off(X, d)})
        peers.append({X: off(X, d), C: 1 - c})
        peers.append({ZH: off(ZH, d)})
        peers.append({ZH: off(ZH, d), ZL: 1 - zl})
        peers.append({Y: off(Y, d)})
        peers.append({Y: off(Y, d), ZL: 1 - zl})
    peers.append({C: 1 - c})
    peers.append({ZL: 1 - zl})
    for p in peers:
        pl.semaphore_signal(barrier, inc=1, device_id=p, device_id_type=MESH)

    for t in range(40):
        tile = pooled_ref[:, 128 * t : 128 * t + 128].T
        done = 0
        while done < 128:
            f = 128 * t + done
            m, r = f // 160, f % 160
            n = min(160 - r, 128 - done)
            pt[(m // 8), m % 2, (m // 2) % 4, r : r + n, :] = tile[done : done + n, :]
            done += n

    def piece(dx, dc):
        xd, cd = off(X, dx), off(C, dc)
        i = dx * 2 + dc
        return remote(pt.at[xd, cd], pr.at[x * 2 + c], sp.at[i], rp.at[x * 2 + c], {X: xd, C: cd})

    def piece_in(xs, csrc):
        return remote(pt.at[0, 0], pr.at[xs * 2 + csrc], sp.at[0], rp.at[xs * 2 + csrc], {C: 1 - c})

    own_piece = pltpu.make_async_copy(pt.at[x, c], pr.at[x * 2 + c], own_sem)
    load_w.wait()
    pre[...] = jnp.zeros_like(pre)

    def tower(k):
        cols = pl.ds(pl.multiple_of(k * 640, 640), 640)
        wk = w_v[pl.ds(k * 5, 5)].reshape(640, 512)
        pre[...] += jnp.dot(pooled_ref[:, cols], wk, preferred_element_type=F32)

    pl.loop(0, 3)(tower)
    pl.semaphore_wait(barrier, len(peers))
    piece(1, 0).start()
    piece(3, 0).start()
    piece(0, 1).start()
    own_piece.start()
    pl.loop(3, 8)(tower)

    pre_act = pre[...] + bias_ref[...]
    sg_ = jax.nn.sigmoid(pre_act)
    slope = sg_ * (1.0 + pre_act * (1.0 - sg_))
    my_rows = pl.ds(pl.multiple_of(c * 128, 128), 128)
    gbuf[x * 4 + zh, my_rows, :] = (gh_ref[...].astype(F32) * slope).astype(BF)

    FIRST, SECOND = (ZH, X), (X, ZH)

    def place(h, al, be):
        return (off(X, be), off(ZH, al)) if h == 0 else (off(X, al), off(ZH, be))

    def half(h, a, b, cc):
        return gbuf.at[a * 4 + b, pl.ds(pl.multiple_of(cc * 128 + h * 64, 64), 64), :]

    def quarter_of(h, q, a, b, cc):
        return gbuf.at[a * 4 + b, pl.ds(pl.multiple_of(cc * 128 + h * 64 + q * 32, 32), 32), :]

    def slot(h, a, b, cc):
        return rg.at[h, a * 8 + b * 2 + cc]

    def qslot(h, q, a, b, cc):
        return (rh if q else rg).at[h, a * 8 + b * 2 + cc]

    def send(h, al, stage, sign):
        a, b = place(h, al, 0)
        ref = half(h, a, b, c)
        axis = (FIRST, SECOND)[stage][h]
        sem = sa.at[h, sign] if stage == 0 else sb.at[h, al * 4 + sign]
        return remote(ref, ref, sem, slot(h, a, b, c), {axis: off(axis, (1, 3)[sign])})

    def onward(h, al, stage, q):
        a, b = place(h, 3 - 2 * q, 0) if stage == 0 else place(h, al, 3 - 2 * q)
        ref = quarter_of(h, q, a, b, c)
        axis = (FIRST, SECOND)[stage][h]
        sem = sa.at[h, 2 + q] if stage == 0 else sb.at[h, al * 4 + 2 + q]
        return remote(ref, ref, sem, qslot(h, q, a, b, c), {axis: off(axis, (1, 3)[q])})

    def to_core(h, al, be):
        a, b = place(h, al, be)
        ref = half(h, a, b, c)
        return remote(ref, ref, sc.at[h, al * 4 + be], slot(h, a, b, c), {C: 1 - c})

    def arrive(h, al, be, dc):
        a, b = place(h, al, be)
        cc = off(C, dc)
        if dc == 0 and (be == 2 or (be == 0 and al == 2)):
            for q in (0, 1):
                ref = quarter_of(h, q, a, b, cc)
                remote(ref, ref, sa.at[0, 0], qslot(h, q, a, b, cc), {C: 1 - c}).wait_recv()
        else:
            ref = half(h, a, b, cc)
            remote(ref, ref, sa.at[0, 0], slot(h, a, b, cc), {C: 1 - c}).wait_recv()

    def process(al, be):
        for h in (1, 0):
            arrive(h, al, be, 0)
            if be == 0:
                if al != 2:
                    onward(h, al, 0, 1 if al == 1 else 0).start()
                for sign in (0, 1):
                    send(h, al, 1, sign).start()
            elif be != 2:
                onward(h, al, 1, 1 if be == 1 else 0).start()
            to_core(h, al, be).start()

    for h in (1, 0):
        for sign in (0, 1):
            send(h, 0, 0, sign).start()
    for h in (1, 0):
        for sign in (0, 1):
            send(h, 0, 1, sign).start()
    for h in (0, 1):
        to_core(h, 0, 0).start()
    for i in ((1, 1), (3, 1), (2, 0), (2, 1)):
        piece(*i).start()

    me = x * 8 + zh * 2 + c

    def find(ref, label):
        return lax.fori_loop(0, 32, lambda i, at: jnp.where(ref[0, i] == me, label(i), at), 0)

    whole_t = find(owner_ref, lambda i: i)
    split_t = find(sowner_ref, lambda i: 32 + i // CS)
    split_c = find(sowner_ref, lambda i: i // CS)
    wtct[:, :128] = w_v[whole_t].T
    wtct[:, 128:] = w_v[split_t].T
    load_keys.wait()
    keys_c[...] = lks_ref[split_c]

    def count_block(keys, out, cols):
        lo = jnp.bitwise_and(keys, 127)
        field = jnp.left_shift(1, jnp.right_shift(keys, 7) * 4)
        sub = lax.broadcasted_iota(jnp.int32, (128, 128), 0)
        packed = jnp.zeros((128, 128), jnp.int32)
        for p in range(8):
            packed += jnp.where(lo[p : p + 1, :] == sub, field[p : p + 1, :], 0)
        for h in range(8):
            n = jnp.bitwise_and(jnp.right_shift(packed, 4 * h), 15)
            out[h * 128 : h * 128 + 128, cols] = n.astype(F32).astype(BF)

    def count(k, carry=None):
        cols = pl.ds(pl.multiple_of(k * 128, 128), 128)
        count_block(lkw_ref[:, cols], cw, cols)
        count_block(keys_c[:, cols], cs, cols)

    steps = [(1, 0), (3, 0), (0, 1), (0, 3), (2, 0), (0, 2)]
    for i, (al, be) in enumerate(steps):
        pl.loop(i * 5, i * 5 + 5)(lambda k: count(k))
        process(al, be)

    pl.loop(30, 32)(lambda k: count(k))

    own_piece.wait()
    for i in range(1, 8):
        piece_in(off(X, i // 2), off(C, i % 2)).wait_recv()
    for d in range(4):
        arrive(0, 0, d, 1)
        arrive(1, d, 0, 1)

    def along_y(d, q):
        yd = off(Y, d)
        return remote(pp.at[yd, q], yr.at[y, q], sy.at[d - 1, q], ry.at[y, q], {Y: yd})

    def from_y(d, q):
        ys = off(Y, d)
        return remote(pp.at[ys, q], yr.at[ys, q], sy.at[0, q], ry.at[ys, q], {Y: ys})

    def bias_y(d):
        return remote(bs, by.at[y], sby.at[d - 1], rby.at[y], {Y: off(Y, d)})

    def bias_from_y(d):
        ys = off(Y, d)
        return remote(bs, by.at[ys], sby.at[0], rby.at[ys], {Y: ys})

    for dz in (1, 3, 2, 0):
        q = off(ZH, dz)
        total = jnp.zeros((160, 512), F32)
        for xs in range(4):
            both = jnp.concatenate([pr[2 * xs, q], pr[2 * xs + 1, q]], axis=1)
            total += jnp.dot(both, gbuf[xs * 4 + zh], preferred_element_type=F32)
        low = total.astype(BF)
        for j in range(4):
            pp[j, q] = low[:, 128 * j : 128 * j + 128]
        for d in (1, 3, 2):
            along_y(d, q).start()

    col = jnp.zeros((8, 512), F32)
    for xs in range(4):
        col += jnp.dot(jnp.ones((8, 256), BF), gbuf[xs * 4 + zh], preferred_element_type=F32)
    bs[...] = jnp.zeros_like(bs)
    for j in range(4):
        bs[j : j + 1, :] = col[0:1, 128 * j : 128 * j + 128]
    for d in (1, 3, 2):
        bias_y(d).start()

    accw[...] = jnp.zeros_like(accw)
    accs[...] = jnp.zeros_like(accs)

    def tables(da, db):
        cb = off(X, da) * 4 + off(ZH, db)
        rows = gbuf[cb]
        cols = pl.ds(pl.multiple_of(cb * 256, 256), 256)
        back = jnp.dot(rows, wtct[...], preferred_element_type=F32).astype(BF)
        accw[...] += jnp.dot(cw[:, cols], back[:, :128], preferred_element_type=F32)
        accs[...] += jnp.dot(cs[:, cols], back[:, 128:], preferred_element_type=F32)

    def other_core(da, db):
        if db:
            arrive(0, db, da, 1)
            arrive(1, da, db, 1)

    process(1, 1)
    tables(0, 0)
    process(1, 3)
    tables(1, 0)
    process(3, 1)
    tables(3, 0)
    process(3, 3)
    tables(2, 0)
    process(2, 1)
    other_core(0, 1)
    tables(0, 1)
    process(2, 3)
    other_core(0, 3)
    tables(0, 3)

    zme = zh * 2 + zl
    others = [(1, 0), (1, 1), (3, 0), (3, 1), (2, 0), (2, 1), (0, 1)]

    def along_z(i):
        zd, ld = off(ZH, others[i][0]), off(ZL, others[i][1])
        return remote(zs.at[zd * 2 + ld], zr.at[zme], sz.at[i], rz.at[zme], {ZH: zd, ZL: ld})

    def from_z(i):
        s = off(ZH, others[i][0]) * 2 + off(ZL, others[i][1])
        return remote(zs.at[s], zr.at[s], sz.at[0], rz.at[s], {C: 1 - c})

    def bias_z(i):
        zd, ld = off(ZH, others[i][0]), off(ZL, others[i][1])
        return remote(bt, bz.at[zme], sbz.at[i], rbz.at[zme], {ZH: zd, ZL: ld})

    def bias_from_z(i):
        s = off(ZH, others[i][0]) * 2 + off(ZL, others[i][1])
        return remote(bt, bz.at[s], sbz.at[0], rbz.at[s], {C: 1 - c})

    for dz in (1, 3, 2, 0):
        q = off(ZH, dz)
        for d in (1, 3, 2):
            from_y(d, q).wait_recv()
        total = pp[y, q].astype(F32)
        for d in (1, 2, 3):
            total += yr[off(Y, d), q].astype(F32)
        zs[q * 2] = total[:80].astype(BF)
        zs[q * 2 + 1] = total[80:].astype(BF)
        for i in range(7):
            if others[i][0] == dz:
                along_z(i).start()

    for d in (1, 3, 2):
        bias_from_y(d).wait_recv()
    col = bs[...]
    for d in (1, 2, 3):
        col += by[off(Y, d)]
    bt[...] = col
    for i in range(7):
        bias_z(i).start()

    process(1, 2)
    other_core(0, 2)
    tables(0, 2)
    process(3, 2)
    for da, db in ((1, 1), (1, 3), (3, 1)):
        other_core(da, db)
        tables(da, db)
    process(2, 2)

    for i in range(7):
        from_z(i).wait_recv()
    total = zs[zme].astype(F32)
    for i in range(7):
        total += zr[off(ZH, others[i][0]) * 2 + off(ZL, others[i][1])].astype(F32)

    gme = y * 2 + zl
    gr[gme] = total.astype(BF)
    group = [(1, 0), (3, 0), (0, 1), (1, 1), (3, 1), (2, 0), (2, 1)]

    def give(i):
        yd, ld = off(Y, group[i][0]), off(ZL, group[i][1])
        return remote(gr.at[gme], gr.at[gme], sg.at[i], rgf.at[gme], {Y: yd, ZL: ld})

    def take(i):
        g = off(Y, group[i][0]) * 2 + off(ZL, group[i][1])
        return remote(gr.at[g], gr.at[g], sg.at[0], rgf.at[g], {C: 1 - c})

    for i in range(7):
        give(i).start()

    for da, db in ((3, 3), (2, 1), (1, 2), (2, 3), (3, 2), (2, 2)):
        other_core(da, db)
        tables(da, db)

    for i in range(7):
        bias_from_z(i).wait_recv()
    col = bt[...]
    for i in range(7):
        col += bz[off(ZH, others[i][0]) * 2 + off(ZL, others[i][1])]
    for j in range(4):
        gb_ref[0:1, 128 * j : 128 * j + 128] = col[j : j + 1, :]

    for i in range(7):
        take(i).wait_recv()
    for yy in range(4):
        for ll in range(2):
            gf_ref[80 * ll : 80 * ll + 80, 128 * yy : 128 * yy + 128] = gr[yy * 2 + ll].astype(F32)
    for i in range(1, 8):
        piece(i // 2, i % 2).wait_send()
    for h in (0, 1):
        for sign in (0, 1):
            send(h, 0, 0, sign).wait_send()
            onward(h, 0, 0, sign).wait_send()
        for al in range(4):
            for sign in (0, 1):
                send(h, al, 1, sign).wait_send()
                onward(h, al, 1, sign).wait_send()
            for be in range(4):
                to_core(h, al, be).wait_send()

    for d in (1, 2, 3):
        for q in range(4):
            along_y(d, q).wait_send()
        bias_y(d).wait_send()
    for i in range(7):
        along_z(i).wait_send()
        bias_z(i).wait_send()
        give(i).wait_send()


def update(
    sowner_ref, gfi_ref, gbi_ref, gw_ref, gs_ref, tw_ref, aw_ref, ts_ref, as_ref,
    gf_ref, gb_ref, nw_ref, ns_ref,
):
    me = lax.axis_index(X) * 8 + lax.axis_index(ZH) * 2 + lax.axis_index(C)
    shard = lax.fori_loop(0, 32, lambda i, at: jnp.where(sowner_ref[0, i] == me, i, at), 0)
    split_c = lax.div(shard, CS)
    quarter = lax.rem(shard, CS)
    gf_ref[...] = gfi_ref[...]
    gb_ref[...] = gbi_ref[...]
    grad = gw_ref[...].T
    square = jnp.sum(grad * grad, axis=0, keepdims=True)
    scale = LEARN_RATE / (jnp.sqrt(aw_ref[...] + square / E) + EPSILON)
    nw_ref[...] = tw_ref[...] - grad * scale
    grads = gs_ref[...].T
    squares = jnp.sum(grads * grads, axis=0, keepdims=True)
    tab = lax.broadcasted_iota(jnp.int32, (8, 1024), 0)
    state = jnp.sum(jnp.where(tab == split_c, as_ref[...], 0.0), axis=0, keepdims=True)
    scales = LEARN_RATE / (jnp.sqrt(state + squares / E) + EPSILON)
    mine = grads[:COLS]
    for q in range(1, CS):
        mine = jnp.where(quarter == q, grads[q * COLS : (q + 1) * COLS], mine)
    ns_ref[...] = ts_ref[...] - mine * scales


VM = pl.BlockSpec(memory_space=pltpu.VMEM)
SM = pl.BlockSpec(memory_space=pltpu.SMEM)
ANY = pl.BlockSpec(memory_space=pl.ANY)
DMA = pltpu.SemaphoreType.DMA


def per_device(
    pooled, grad_hidden, w_first, bias_first, table_owner, shard_owner, lookups_whole,
    lookups_split, table_whole, accum_whole, table_split, accum_split,
):
    keys_whole = jnp.swapaxes(lookups_whole[0, 0], 0, 1)
    keys_split = jnp.swapaxes(lookups_split[0], 1, 2)
    grad_first, grad_bias, grad_whole, grad_split = pl.pallas_call(
        kernel,
        out_shape=(
            jax.ShapeDtypeStruct((160, 512), F32),
            jax.ShapeDtypeStruct((1, 512), F32),
            jax.ShapeDtypeStruct((1024, 128), F32),
            jax.ShapeDtypeStruct((1024, 128), F32),
        ),
        in_specs=[SM, SM, VM, VM, ANY, VM, VM, ANY],
        out_specs=(VM, VM, VM, VM),
        scratch_shapes=[
            pltpu.VMEM((40, 128, 512), BF),
            pltpu.VMEM((8, 8, 4096), jnp.int32),
            pltpu.VMEM((4, 2, 4, 160, 128), BF),
            pltpu.VMEM((8, 4, 160, 128), BF),
            pltpu.VMEM((16, 256, 512), BF),
            pltpu.VMEM((4, 4, 160, 128), BF),
            pltpu.VMEM((4, 4, 160, 128), BF),
            pltpu.VMEM((8, 80, 128), BF),
            pltpu.VMEM((8, 80, 128), BF),
            pltpu.VMEM((8, 128), F32),
            pltpu.VMEM((4, 8, 128), F32),
            pltpu.VMEM((8, 128), F32),
            pltpu.VMEM((8, 8, 128), F32),
            pltpu.VMEM((1024, 4096), BF),
            pltpu.VMEM((1024, 4096), BF),
            pltpu.VMEM((512, 256), BF),
            pltpu.VMEM((128, 512), F32),
            pltpu.VMEM((8, 4096), jnp.int32),
            pltpu.VMEM((8, 80, 128), BF),
            DMA,
            DMA,
            DMA,
            DMA((8,)), DMA((8,)),
            DMA((2, 4)), DMA((2, 16)), DMA((2, 16)), DMA((2, 32)), DMA((2, 32)),
            DMA((3, 4)), DMA((4, 4)),
            DMA((7,)), DMA((8,)),
            DMA((7,)), DMA((8,)),
            DMA((3,)), DMA((4,)),
            DMA((7,)), DMA((8,)),
        ],
        compiler_params=pltpu.CompilerParams(
            collective_id=0, has_side_effects=True, vmem_limit_bytes=58 * 2**20
        ),
        name="step",
    )(
        table_owner, shard_owner, pooled, grad_hidden, w_first.reshape(40, 128, 512), bias_first[None],
        keys_whole, keys_split,
    )
    grad_first, grad_bias, new_whole, new_split = pl.pallas_call(
        update,
        out_shape=(
            jax.ShapeDtypeStruct((160, 512), F32),
            jax.ShapeDtypeStruct((1, 512), F32),
            jax.ShapeDtypeStruct((128, 1024), F32),
            jax.ShapeDtypeStruct((32, 1024), F32),
        ),
        in_specs=[SM, VM, VM, VM, VM, VM, VM, VM, VM],
        out_specs=(VM, VM, VM, VM),
        name="update",
    )(
        shard_owner, grad_first, grad_bias, grad_whole, grad_split,
        table_whole[0, 0], accum_whole[0], table_split[0, 0], accum_split[0],
    )
    return grad_first, grad_bias[0], new_whole[None, None], new_split[None, None]


def solution(mesh):
    finer = Mesh(mesh.devices.reshape(2, 4, 4, 4, 2), GRP_MEM)
    in_specs = (
        P(GRP_MEM, None),
        P(GRP_MEM, None),
        P(),
        P(),
        P(GRP, None),
        P(GRP, None),
        P(GRP, MEM, None, None),
        P(GRP, None, None, None),
        P(GRP, MEM, None, None),
        P(GRP, MEM, None),
        P(GRP, MEM, None, None),
        P(GRP, None, None),
    )
    out_specs = (P(MEM, None), P(), P(GRP, MEM, None, None), P(GRP, MEM, None, None))
    return jax.shard_map(
        per_device, mesh=finer, in_specs=in_specs, out_specs=out_specs, check_vma=False
    )
```

time: 70.5 us -> 62.7 us (0.89)
  local copies, waits for them, and re-layouts: 6.42 us -> 0 us
  Pallas kernels: 63.2 us -> 61.9 us
    unnamed x4 -> x0, local copies, waits for them, and re-layouts: 6.42 us -> none
    pallas_call x1, Pallas kernels: 63.2 us -> 58.7 us  [per_device(): pl.pallas_call(kernel, out_shape=(jax.ShapeDtypeStruct((160, 512), F32),...]
    pallas_call x0 -> x1, Pallas kernels: none -> 3.16 us  [per_device(): pl.pallas_call(update, out_shape=(jax.ShapeDtypeStruct((160, 512), F32),...]
where the time goes in v2:
time: 62.7 us; the launch traced here: 62.5 us
  Pallas kernels  61.9 us (99%)
  between operations  0.64 us (1%)
    pallas_call x1, Pallas kernels, per_device(): pl.pallas_call(kernel, out_shape=(jax.ShapeDtypeStruct((160, 512), F32),...  58.7 us
    pallas_call x1, Pallas kernels, per_device(): pl.pallas_call(update, out_shape=(jax.ShapeDtypeStruct((160, 512), F32),...  3.16 us

profile of v2, /device:TPU:1, one launch (start us, length us, event | category | flops | bytes accessed | tf_op | source)
XLA Modules:
  0.0 62.5 jit_solution(8538192516685824964)
XLA Ops:
  0.6 58.7 %step.1 = (f32[160,512]{1,0:T(8,128)}, f32[1,512]{1,0:T(1,128)}, f32[1024,128]{1,0:T(8,128)}, f32[1024,128]{1,0:T(8,128)}) custom-call(s32[1,32]{1,0:T(1,128)} %owner_ref.1, s32[1,32]{1,0:T(1,128)} %sowner_ref.3, bf16[128,5120]{1,0:T(8,128)(2,1)} %pooled_ref.1, bf16[128,512]{1,0:T(8,128)(2,1)} %gh_ref.1, bf16[40,128,512]{2,1,0:T(8,128)(2,1)} %bitcast.15, ...), custom_call_target="tpu_custom_call" | custom-call | tf_op jit(solution)/shard_map/step/pallas_call | solution.py:430
  59.4 3.2 %update.1 = (f32[160,512]{1,0:T(8,128)}, f32[1,512]{1,0:T(1,128)}, f32[128,1024]{1,0:T(8,128)}, f32[32,1024]{1,0:T(8,128)}) custom-call(s32[1,32]{1,0:T(1,128)} %sowner_ref.3, f32[160,512]{1,0:T(8,128)} %get-tuple-element.12.gfi_ref, f32[1,512]{1,0:T(1,128)} %get-tuple-element.13.gbi_ref, f32[1024,128]{1,0:T(8,128)} %get-tuple-element.14.gw_ref, ...), custom_call_target="tpu_custom_call" | custom-call | tf_op jit(solution)/shard_map/update/pallas_call | solution.py:479

commit v3 on v2

--- a/solution.py
+++ b/solution.py
@@ -8,6 +8,7 @@
 
 E = 128
 CS = 4
+NEAR = 96
 COLS = 32
 ZL, Y, X, ZH, C = "grp_0", "grp_1", "mem_0", "mem_1", "mem_2"
 SIZE = {ZL: 2, Y: 4, X: 4, ZH: 4, C: 2}
@@ -105,10 +106,12 @@
         return (off(X, be), off(ZH, al)) if h == 0 else (off(X, al), off(ZH, be))
 
     def half(h, a, b, cc):
-        return gbuf.at[a * 4 + b, pl.ds(pl.multiple_of(cc * 128 + h * 64, 64), 64), :]
+        start, rows = ((0, NEAR), (NEAR, 128 - NEAR))[h]
+        return gbuf.at[a * 4 + b, pl.ds(pl.multiple_of(cc * 128 + start, 16), rows), :]
 
     def quarter_of(h, q, a, b, cc):
-        return gbuf.at[a * 4 + b, pl.ds(pl.multiple_of(cc * 128 + h * 64 + q * 32, 32), 32), :]
+        start, rows = ((0, NEAR // 2), (NEAR, 64 - NEAR // 2))[h]
+        return gbuf.at[a * 4 + b, pl.ds(pl.multiple_of(cc * 128 + start + q * rows, 16), rows), :]
 
     def slot(h, a, b, cc):
         return rg.at[h, a * 8 + b * 2 + cc]
@@ -146,8 +149,8 @@
             ref = half(h, a, b, cc)
             remote(ref, ref, sa.at[0, 0], slot(h, a, b, cc), {C: 1 - c}).wait_recv()
 
-    def process(al, be):
-        for h in (1, 0):
+    def process(*steps):
+        for h, al, be in steps:
             arrive(h, al, be, 0)
             if be == 0:
                 if al != 2:
@@ -198,12 +201,15 @@
         count_block(lkw_ref[:, cols], cw, cols)
         count_block(keys_c[:, cols], cs, cols)
 
-    steps = [(1, 0), (3, 0), (0, 1), (0, 3), (2, 0), (0, 2)]
-    for i, (al, be) in enumerate(steps):
-        pl.loop(i * 5, i * 5 + 5)(lambda k: count(k))
-        process(al, be)
-
-    pl.loop(30, 32)(lambda k: count(k))
+    steps = [
+        (1, 1, 0), (0, 0, 1), (1, 3, 0), (0, 0, 3), (0, 1, 0), (1, 0, 1), (0, 3, 0), (1, 0, 3),
+        (0, 2, 0), (1, 0, 2), (1, 1, 1), (1, 1, 3), (1, 3, 1), (1, 3, 3), (1, 1, 2), (1, 3, 2),
+    ]
+    for i, step in enumerate(steps):
+        pl.loop(i * 2, i * 2 + 2)(lambda k: count(k))
+        process(step)
+
+    process((1, 2, 0), (0, 0, 2))
 
     own_piece.wait()
     for i in range(1, 8):
@@ -264,20 +270,24 @@
             arrive(0, db, da, 1)
             arrive(1, da, db, 1)
 
-    process(1, 1)
+    process((0, 1, 1))
     tables(0, 0)
-    process(1, 3)
+    process((0, 3, 1))
     tables(1, 0)
-    process(3, 1)
+    process((1, 2, 1))
     tables(3, 0)
-    process(3, 3)
+    process((0, 1, 3))
     tables(2, 0)
-    process(2, 1)
+    process((0, 3, 3))
     other_core(0, 1)
     tables(0, 1)
-    process(2, 3)
+    process((1, 2, 3))
     other_core(0, 3)
     tables(0, 3)
+    process((0, 2, 1))
+    other_core(0, 2)
+    tables(0, 2)
+    process((0, 2, 3))
 
     zme = zh * 2 + zl
     others = [(1, 0), (1, 1), (3, 0), (3, 1), (2, 0), (2, 1), (0, 1)]
@@ -320,14 +330,15 @@
     for i in range(7):
         bias_z(i).start()
 
-    process(1, 2)
-    other_core(0, 2)
-    tables(0, 2)
-    process(3, 2)
-    for da, db in ((1, 1), (1, 3), (3, 1)):
-        other_core(da, db)
-        tables(da, db)
-    process(2, 2)
+    process((0, 1, 2))
+    other_core(1, 1)
+    tables(1, 1)
+    process((0, 3, 2))
+    other_core(1, 3)
+    tables(1, 3)
+    process((1, 2, 2), (0, 2, 2))
+    other_core(3, 1)
+    tables(3, 1)
 
     for i in range(7):
         from_z(i).wait_recv()

time: 62.7 us -> 60.4 us (0.963)
  Pallas kernels: 61.9 us -> 59.7 us
    pallas_call x1, Pallas kernels: 58.7 us -> 56.5 us  [per_device(): pl.pallas_call(kernel, out_shape=(jax.ShapeDtypeStruct((160, 512), F32),...]
where the time goes in v3:
time: 60.4 us; the launch traced here: 60.3 us
  Pallas kernels  59.7 us (99%)
  between operations  0.64 us (1%)
    pallas_call x1, Pallas kernels, per_device(): pl.pallas_call(kernel, out_shape=(jax.ShapeDtypeStruct((160, 512), F32),...  56.5 us
    pallas_call x1, Pallas kernels, per_device(): pl.pallas_call(update, out_shape=(jax.ShapeDtypeStruct((160, 512), F32),...  3.16 us

profile of v3, /device:TPU:1, one launch (start us, length us, event | category | flops | bytes accessed | tf_op | source)
XLA Modules:
  0.0 60.3 jit_solution(1099303533581135769)
XLA Ops:
  0.6 56.5 %step.1 = (f32[160,512]{1,0:T(8,128)}, f32[1,512]{1,0:T(1,128)}, f32[1024,128]{1,0:T(8,128)}, f32[1024,128]{1,0:T(8,128)}) custom-call(s32[1,32]{1,0:T(1,128)} %owner_ref.1, s32[1,32]{1,0:T(1,128)} %sowner_ref.3, bf16[128,5120]{1,0:T(8,128)(2,1)} %pooled_ref.1, bf16[128,512]{1,0:T(8,128)(2,1)} %gh_ref.1, bf16[40,128,512]{2,1,0:T(8,128)(2,1)} %bitcast.15, ...), custom_call_target="tpu_custom_call" | custom-call | tf_op jit(solution)/shard_map/step/pallas_call | solution.py:441
  57.1 3.2 %update.1 = (f32[160,512]{1,0:T(8,128)}, f32[1,512]{1,0:T(1,128)}, f32[128,1024]{1,0:T(8,128)}, f32[32,1024]{1,0:T(8,128)}) custom-call(s32[1,32]{1,0:T(1,128)} %sowner_ref.3, f32[160,512]{1,0:T(8,128)} %get-tuple-element.12.gfi_ref, f32[1,512]{1,0:T(1,128)} %get-tuple-element.13.gbi_ref, f32[1024,128]{1,0:T(8,128)} %get-tuple-element.14.gw_ref, ...), custom_call_target="tpu_custom_call" | custom-call | tf_op jit(solution)/shard_map/update/pallas_call | solution.py:490
